TPU v7x, 32 devices: a whole 2x2x4 slice. The times are simulated.
32 devices in a mesh: row: 4 (over y, x), col: 4 (over z), vox: 2 (over core).
Axes of the slice: x: 2, y: 2, z: 4, core: 2. Of those that a mesh axis runs over, the one named last changes fastest.
Arguments:
- coeffs_r: bfloat16 [32, 4, 64, 2, 1024], P(None, 'row', None, None, 'col'), may hold values from -0.125 to 0.125
- rhs: bfloat16 [32, 4, 64, 1536], P('col', 'row', None, 'vox'), may hold values from -6 to 6
- inverses: bfloat16 [2, 1024, 1024], replicated, may hold values from -0.1875 to 0.1875
Outputs:
- updated: bfloat16 [32, 4, 64, 1536], P('col', 'row', None, 'vox')
All inputs are finite; a program needn't handle non-finite values.
Results may differ from a plain program's by a relative error of at most 0.0049.
Values may be sent and summed in bfloat16 or wider, within the bound.
No kernel may reach another device: no remote copies, remote signals or barrier semaphores. Data moves between devices by JAX's collectives and lax.ppermute only.
A program may use at most 64 MiB of HBM per device.

v0:
```python
import jax
import jax.numpy as jnp
from jax import lax
from jax.sharding import PartitionSpec as P


def spread(value, axis, root):
    mine = lax.axis_index(axis) == root
    return lax.psum(jnp.where(mine, value, jnp.zeros_like(value)), axis)


def solve_block(inverse, rhs_block, col_pos, own_cols):
    solved_all = jnp.dot(inverse, rhs_block, preferred_element_type=jnp.float32).astype(
        jnp.bfloat16
    )
    solved_mine = lax.dynamic_slice_in_dim(solved_all, col_pos * own_cols, own_cols, 0)
    return (solved_all, solved_mine)


def local(coeffs_r, rhs, inverses):
    row_count = lax.axis_size("row")
    col_count = lax.axis_size("col")
    row_pos = lax.axis_index("row")
    col_pos = lax.axis_index("col")
    per_col = rhs.shape[0]
    block_rows = rhs.shape[2]
    voxels = rhs.shape[3]
    cycles = coeffs_r.shape[0]
    own_cols = coeffs_r.shape[4]
    block_order = inverses.shape[1]
    tail_cycles = block_order // (block_rows * row_count)
    owner_col = col_count - 1
    tail_piece = rhs[per_col - tail_cycles :]
    tail_rows = lax.all_gather(tail_piece, "row", axis=1, tiled=True)
    tail_rows = spread(tail_rows, "col", owner_col)
    solved_last, last_mine = solve_block(
        inverses[1], tail_rows.reshape(block_order, voxels), col_pos, own_cols
    )
    panel_rows = coeffs_r[cycles - 2 * tail_cycles : cycles - tail_cycles, 0, :, 1, :]
    panel_rows = panel_rows.reshape(tail_cycles * block_rows, own_cols)
    partial_value = -jnp.dot(panel_rows, last_mine, preferred_element_type=jnp.float32)
    known = rhs[per_col - 2 * tail_cycles : per_col - tail_cycles, 0]
    known = known.reshape(tail_cycles * block_rows, voxels).astype(jnp.float32)
    partial_value = partial_value + jnp.where(col_pos == owner_col, known, jnp.zeros_like(known))
    partial_value = partial_value.reshape(tail_cycles, 1, block_rows, voxels)
    padded = jnp.zeros((tail_cycles, row_count, block_rows, voxels), jnp.float32)
    anchor = jnp.zeros((), jnp.int32)
    padded = lax.dynamic_update_slice(padded, partial_value, (anchor, row_pos, anchor, anchor))
    middle_rhs = lax.psum(padded, ("row", "col")).astype(jnp.bfloat16)
    solved_first, first_mine = solve_block(
        inverses[0], middle_rhs.reshape(block_order, voxels), col_pos, own_cols
    )
    stacked_all = jnp.stack([solved_first, solved_last])
    removed = jnp.einsum(
        "kprjc,jcv->kprv",
        lax.all_to_all(coeffs_r, "col", split_axis=0, concat_axis=4, tiled=True),
        stacked_all,
        preferred_element_type=jnp.float32,
    )
    remaining = (rhs.astype(jnp.float32) - removed).astype(jnp.bfloat16)

    def my_rows(solved):
        shaped = solved.reshape(tail_cycles, row_count, block_rows, voxels)
        return lax.dynamic_slice_in_dim(shaped, row_pos, 1, 1)

    window = jnp.concatenate([my_rows(solved_first), my_rows(solved_last)], 0)
    lower_part = jnp.where(col_pos == owner_col, window, remaining[per_col - 2 * tail_cycles :])
    return jnp.concatenate([remaining[: per_col - 2 * tail_cycles], lower_part], 0)


def solution(mesh):
    placed = (P(None, "row", None, None, "col"), P("col", "row", None, "vox"), P())
    return jax.shard_map(
        local, mesh=mesh, in_specs=placed, out_specs=P("col", "row", None, "vox"), check_vma=False
    )
```

profile of v0, /device:TPU:0, one launch (start us, length us, event | category | flops | bytes accessed | tf_op | source)
XLA Modules:
  0.0 290.5 jit_solution(9024316782090416812)
XLA Ops:
  6.5 0.0 all-gather.2.cloned.1.call-start
  6.5 1.8 slice.15
  8.3 0.0 all-gather.2.cloned.1.call-update
  8.3 6.4 %all-to-all-start = ((bf16[32,1,64,2,256]{4,3,2,1,0:T(2,128)(2,1)}), bf16[32,1,64,2,256]{4,3,2,1,0:T(2,128)(2,1)S(1)}, u32[]{:S(2)}, u32[]{:S(2)}) async-start(bf16[32,1,64,2,256]{4,3,2,1,0:T(2,128)(2,1)} %param.3), calls=%async_computation | async-start | bytes 4194304 | tf_op jit(solution)/shard_map/all_to_all | solution.py:56
  14.7 0.0 all-reduce.3.cloned.1.call-start
  14.7 28.1 %all-gather.2.cloned.1.call-done = bf16[4,4,64,768]{3,2,1,0:T(8,128)(2,1)} async-done(((bf16[4,1,64,768]{3,2,1,0:T(8,128)(2,1)}), bf16[4,4,64,768]{3,2,1,0:T(8,128)(2,1)}) %all-gather.2.cloned.1.call-update) | async-done | bytes 1572880 | tf_op jit(solution)/shard_map/all_gather | solution.py:34
  42.8 1.3 broadcast_select_fusion
  44.1 0.0 all-reduce.3.cloned.1.call-update
  44.1 1.2 slice.17
  45.4 1.1 convert_select_fusion
  46.4 39.1 %all-to-all-done = bf16[32,1,64,2,256]{4,3,2,1,0:T(2,128)(2,1)S(1)} async-done(((bf16[32,1,64,2,256]{4,3,2,1,0:T(2,128)(2,1)}), bf16[32,1,64,2,256]{4,3,2,1,0:T(2,128)(2,1)S(1)}, u32[]{:S(2)}, u32[]{:S(2)}) %all-to-all-start) | async-done | bytes 2097184 | tf_op jit(solution)/shard_map/all_to_all | solution.py:56
  85.5 2.9 %copy.27 = bf16[4,8,1,64,2,256]{5,0,3,4,1,2:T(4,128)(2,1)} copy(bf16[4,8,1,64,2,256]{5,4,3,1,0,2:T(2,128)(2,1)S(1)} %bitcast.69) | data formatting | bytes 4194304 | tf_op jit(solution)/shard_map/all_to_all | solution.py:56
  88.5 4.4 %reshape.29 = bf16[8,64,2,1024]{3,1,2,0:T(8,128)(2,1)} reshape(bf16[8,1,64,2,4,256]{5,4,2,3,0,1:T(4,128)(2,1)} %bitcast.70) | data formatting | bytes 4194304 | tf_op jit(solution)/shard_map/reshape
  92.9 30.7 %all-reduce.3.cloned.1.call-done = bf16[1024,768]{1,0:T(8,128)(2,1)} async-done(((bf16[1024,768]{1,0:T(8,128)(2,1)}), bf16[1024,768]{1,0:T(8,128)(2,1)}) %all-reduce.3.cloned.1.call-update) | async-done | bytes 1572880 | tf_op jit(solution)/shard_map/psum | solution.py:9
  123.6 3.9 %fusion.9 = bf16[768,1024]{1,0:T(8,128)(2,1)S(1)} fusion(bf16[1024,768]{1,0:T(8,128)(2,1)} %all-reduce.3.cloned.1.call-done, bf16[2,1024,1024]{2,1,0:T(8,128)(2,1)} %param.5), kind=kOutput, calls=%fused_computation.11 | convolution fusion | flops 1611399168 | bytes 5242880 | tf_op jit(solution)/shard_map/dot_general | solution.py:13
  127.5 0.0 copy-start
  127.5 0.3 fusion.17
  127.9 0.3 broadcast_in_dim.9
  128.2 0.5 copy-done
  128.7 0.1 constant_dynamic-update-slice_fusion
  128.7 142.3 %all-reduce.4 = bf16[4,4,64,768]{3,2,1,0:T(8,128)(2,1)} all-reduce(f32[4,4,64,768]{3,2,1,0:T(8,128)S(1)} %constant_dynamic-update-slice_fusion), channel_id=1, replica_groups=mesh['row'=4,'col'=4,'vox'=2] {'row','col'}, use_global_device_ids=true, to_apply=%region_1.2 | all-reduce | flops 786432 | bytes 4718592 | tf_op jit(solution)/shard_map/psum | solution.py:49
  271.0 5.1 %fusion.12 = bf16[768,1024]{1,0:T(8,128)(2,1)} fusion(bf16[1024,768]{1,0:T(8,128)(2,1)} %bitcast.80, bf16[2,1024,1024]{2,1,0:T(8,128)(2,1)} %param.5), kind=kOutput, calls=%fused_computation.12 | convolution fusion | flops 1611399168 | bytes 5242880 | tf_op jit(solution)/shard_map/dot_general | solution.py:13
  276.1 0.0 copy-start.1
  276.1 1.8 copy.12
  277.9 0.0 copy-done.1
  277.9 0.7 copy.14
  278.7 5.0 %fusion.19 = bf16[8,1,64,768]{3,2,1,0:T(8,128)(2,1)} fusion(bf16[8,64,2,1024]{3,1,2,0:T(8,128)(2,1)} %reshape.29, bf16[1,1024,768]{1,2,0:T(8,128)(2,1)S(1)} %bitcast.75, bf16[1,1024,768]{1,2,0:T(8,128)(2,1)} %bitcast.79, bf16[4,1,64,768]{3,2,0,1:T(8,128)(2,1)S(1)} %dynamic-slice_bitcast_fusion, bf16[4,1,64,768]{3,2,0,1:T(8,128)(2,1)S(1)} %dynamic-slice_bitcast_fusion.1, ...), kind=kOutput, calls=%fused_computation.20 | convolution fusion | flops 1618870272 | bytes 7602177 | tf_op jit(solution)/shard_map/kprjc,jcv->kprv/dot_general | solution.py:54
  (3 shorter events, 0.1 us)
Async XLA Ops:
  6.5 36.2 %all-gather.2.cloned.1.call-start = ((), (), s32[]{:S(2)}) async-start(), calls=%async_computation.1 | async-start | bytes 1966080 | tf_op jit(solution)/shard_map/all_gather | solution.py:34
  8.3 77.2 %all-to-all-start = ((bf16[32,1,64,2,256]{4,3,2,1,0:T(2,128)(2,1)}), bf16[32,1,64,2,256]{4,3,2,1,0:T(2,128)(2,1)S(1)}, u32[]{:S(2)}, u32[]{:S(2)}) async-start(bf16[32,1,64,2,256]{4,3,2,1,0:T(2,128)(2,1)} %param.3), calls=%async_computation | async-start | bytes 4194304 | tf_op jit(solution)/shard_map/all_to_all | solution.py:56
  14.7 108.9 %all-reduce.3.cloned.1.call-start = ((), (), s32[]{:S(2)}) async-start(), calls=%async_computation.2 | async-start | bytes 3145728 | tf_op jit(solution)/shard_map/psum | solution.py:9
  127.5 1.1 copy-start
  276.1 1.9 copy-start.1
Sparse Core Ops, SparseCore 0:
  9.2 33.5 all-gather.1
  45.1 78.4 all-reduce.2
where the time goes:
time: 291 us
  blocking collectives  142 us (49%)
  waiting for transfers between devices  97.9 us (34%)
  matrix products  14.3 us (5%)
  local copies, waits for them, and re-layouts  13.9 us (5%)
  between operations  13.5 us (5%)
  starting transfers between devices  6.36 us (2%)
    psum x1, blocking collectives, local(): middle_rhs = lax.psum(padded, ('row', 'col')).astype(jnp.bfloat16)  142 us
    all_to_all x1, waiting for transfers between devices, local(): lax.all_to_all(coeffs_r, 'col', split_axis=0, concat_axis=4, tiled=True)  39.1 us
    psum x1, waiting for transfers between devices, spread(): return lax.psum(jnp.where(mine, value, jnp.zeros_like(value)), axis)  30.7 us
    all_gather x1, waiting for transfers between devices, local(): tail_rows = lax.all_gather(tail_piece, 'row', axis=1, tiled=True)  28.1 us
    dot_general x2, matrix products, solve_block(): jnp.dot(inverse, rhs_block, preferred_element_type=jnp.float32)  8.96 us
    all_to_all x1, starting transfers between devices, local(): lax.all_to_all(coeffs_r, 'col', split_axis=0, concat_axis=4, tiled=True)  6.36 us
  transfers between devices with their start and end apart: 3, of which 3 were waited for; matrix products, arithmetic and copies ran while one was open for 4% of the time, Pallas kernels for 0%

commit v1 on v0

--- a/solution.py
+++ b/solution.py
@@ -6,7 +6,7 @@
 
 def spread(value, axis, root):
     mine = lax.axis_index(axis) == root
-    return lax.psum(jnp.where(mine, value, jnp.zeros_like(value)), axis)
+    return jnp.sum(lax.all_gather(jnp.where(mine, value, jnp.zeros_like(value)), axis), axis=0)
 
 
 def solve_block(inverse, rhs_block, col_pos, own_cols):

time: 291 us -> 370 us (1.27)
  waiting for transfers between devices: 97.9 us -> 174 us
  other arithmetic: 2.35 us -> 6.48 us
    all_to_all x1, waiting for transfers between devices: 39.1 us -> 102 us  [local(): lax.all_to_all(coeffs_r, 'col', split_axis=0, concat_axis=4, tiled=True)]
    all_gather x0 -> x1, waiting for transfers between devices: none -> 37.8 us  [spread(): lax.all_gather(jnp.where(mine, value, jnp.zeros_like(value)), axis)]
    psum x1 -> x0, waiting for transfers between devices: 30.7 us -> none  [spread(): return lax.psum(jnp.where(mine, value, jnp.zeros_like(value)), axis)]
    all_gather x1, waiting for transfers between devices: 28.1 us -> 34.4 us  [local(): tail_rows = lax.all_gather(tail_piece, 'row', axis=1, tiled=True)]
    reduce_sum x0 -> x1, other arithmetic: none -> 4.13 us  [spread(): jnp.sum(lax.all_gather(jnp.where(mine, value, jnp.zeros_like(value)), axi...]
  transfers between devices with their start and end apart: 3 -> 3, of which waited for: 3 -> 3; matrix products, arithmetic and copies ran while one was open for 4% -> 3% of each run, Pallas kernels for 0% -> 0%
where the time goes in v1:
time: 370 us
  waiting for transfers between devices  174 us (47%)
  blocking collectives  142 us (38%)
  local copies, waits for them, and re-layouts  14 us (4%)
  matrix products  13.8 us (4%)
  between operations  13.5 us (4%)
  other arithmetic  6.48 us (2%)
  starting transfers between devices  6.06 us (2%)
    psum x1, blocking collectives, local(): middle_rhs = lax.psum(padded, ('row', 'col')).astype(jnp.bfloat16)  142 us
    all_to_all x1, waiting for transfers between devices, local(): lax.all_to_all(coeffs_r, 'col', split_axis=0, concat_axis=4, tiled=True)  102 us
    all_gather x1, waiting for transfers between devices, spread(): lax.all_gather(jnp.where(mine, value, jnp.zeros_like(value)), axis)  37.8 us
    all_gather x1, waiting for transfers between devices, local(): tail_rows = lax.all_gather(tail_piece, 'row', axis=1, tiled=True)  34.4 us
    dot_general x2, matrix products, solve_block(): jnp.dot(inverse, rhs_block, preferred_element_type=jnp.float32)  8.49 us
  transfers between devices with their start and end apart: 3, of which 3 were waited for; matrix products, arithmetic and copies ran while one was open for 3% of the time, Pallas kernels for 0%

profile of v1, /device:TPU:0, one launch (start us, length us, event | category | flops | bytes accessed | tf_op | source)
XLA Modules:
  0.0 369.7 jit_solution(3191164801924173211)
XLA Ops:
  6.5 0.0 all-gather.4.cloned.1.call-start
  6.5 1.8 slice.15
  8.3 0.0 all-gather.4.cloned.1.call-update
  8.3 0.0 all-gather.6.cloned.1.call-start
  8.4 34.4 %all-gather.4.cloned.1.call-done = bf16[4,4,64,768]{3,2,1,0:T(8,128)(2,1)} async-done(((bf16[4,1,64,768]{3,2,1,0:T(8,128)(2,1)}), bf16[4,4,64,768]{3,2,1,0:T(8,128)(2,1)}) %all-gather.4.cloned.1.call-update) | async-done | bytes 1572880 | tf_op jit(solution)/shard_map/all_gather | solution.py:34
  42.8 1.3 broadcast_select_fusion
  44.0 0.0 all-gather.6.cloned.1.call-update
  44.0 6.0 %all-to-all-start = ((bf16[32,1,64,2,256]{4,3,2,1,0:T(2,128)(2,1)}), bf16[32,1,64,2,256]{4,3,2,1,0:T(2,128)(2,1)S(1)}, u32[]{:S(2)}, u32[]{:S(2)}) async-start(bf16[32,1,64,2,256]{4,3,2,1,0:T(2,128)(2,1)} %param.3), calls=%async_computation | async-start | bytes 4194304 | tf_op jit(solution)/shard_map/all_to_all | solution.py:56
  50.1 1.3 slice.17
  51.4 1.1 convert_select_fusion
  52.5 102.0 %all-to-all-done = bf16[32,1,64,2,256]{4,3,2,1,0:T(2,128)(2,1)S(1)} async-done(((bf16[32,1,64,2,256]{4,3,2,1,0:T(2,128)(2,1)}), bf16[32,1,64,2,256]{4,3,2,1,0:T(2,128)(2,1)S(1)}, u32[]{:S(2)}, u32[]{:S(2)}) %all-to-all-start) | async-done | bytes 2097184 | tf_op jit(solution)/shard_map/all_to_all | solution.py:56
  154.5 3.0 copy.37
  157.5 4.5 %reshape.29 = bf16[8,64,2,1024]{3,1,2,0:T(8,128)(2,1)} reshape(bf16[8,1,64,2,4,256]{5,4,2,3,0,1:T(4,128)(2,1)} %bitcast.71) | data formatting | bytes 4194304 | tf_op jit(solution)/shard_map/reshape
  162.0 37.8 %all-gather.6.cloned.1.call-done = bf16[16,4,64,768]{3,2,1,0:T(8,128)(2,1)} async-done(((bf16[4,4,64,768]{3,2,1,0:T(8,128)(2,1)}), bf16[16,4,64,768]{3,2,1,0:T(8,128)(2,1)}) %all-gather.6.cloned.1.call-update) | async-done | bytes 6291472 | tf_op jit(solution)/shard_map/all_gather | solution.py:9
  199.8 4.1 %reduce_sum.12 = bf16[4,4,64,768]{3,2,1,0:T(8,128)(2,1)S(1)} reduce(bf16[4,4,4,64,768]{4,3,2,1,0:T(8,128)(2,1)} %bitcast.72, bf16[]{:T(256)} %constant.6.clone.1), dimensions={0}, to_apply=%region_0.1 | reduce | flops 2359296 | bytes 7864322 | tf_op jit(solution)/shard_map/reduce_sum | solution.py:9
  203.9 3.4 fusion.9
  207.3 0.0 copy-start
  207.4 0.3 fusion.17
  207.7 0.3 broadcast_in_dim.9
  208.0 0.5 copy-done
  208.5 0.1 constant_dynamic-update-slice_fusion
  208.6 141.6 %all-reduce.1 = bf16[4,4,64,768]{3,2,1,0:T(8,128)(2,1)} all-reduce(f32[4,4,64,768]{3,2,1,0:T(8,128)S(1)} %constant_dynamic-update-slice_fusion), channel_id=1, replica_groups=mesh['row'=4,'col'=4,'vox'=2] {'row','col'}, use_global_device_ids=true, to_apply=%region_1.2 | all-reduce | flops 786432 | bytes 4718592 | tf_op jit(solution)/shard_map/psum | solution.py:49
  350.2 5.1 %fusion.12 = bf16[768,1024]{1,0:T(8,128)(2,1)} fusion(bf16[1024,768]{1,0:T(8,128)(2,1)} %bitcast.81, bf16[2,1024,1024]{2,1,0:T(8,128)(2,1)} %param.5), kind=kOutput, calls=%fused_computation.12 | convolution fusion | flops 1611399168 | bytes 5242880 | tf_op jit(solution)/shard_map/dot_general | solution.py:13
  355.2 0.0 copy-start.1
  355.2 1.8 copy.22
  357.1 0.0 copy-done.1
  357.1 0.7 copy.24
  357.9 5.0 %fusion.19 = bf16[8,1,64,768]{3,2,1,0:T(8,128)(2,1)} fusion(bf16[8,64,2,1024]{3,1,2,0:T(8,128)(2,1)} %reshape.29, bf16[1,1024,768]{1,2,0:T(8,128)(2,1)S(1)} %bitcast.76, bf16[1,1024,768]{1,2,0:T(8,128)(2,1)} %bitcast.80, bf16[4,1,64,768]{3,2,0,1:T(8,128)(2,1)S(1)} %dynamic-slice_bitcast_fusion, bf16[4,1,64,768]{3,2,0,1:T(8,128)(2,1)S(1)} %dynamic-slice_bitcast_fusion.1, ...), kind=kOutput, calls=%fused_computation.20 | convolution fusion | flops 1618870272 | bytes 7602177 | tf_op jit(solution)/shard_map/kprjc,jcv->kprv/dot_general | solution.py:54
  (3 shorter events, 0.1 us)
Async XLA Ops:
  6.5 36.2 %all-gather.4.cloned.1.call-start = ((), (), s32[]{:S(2)}) async-start(), calls=%async_computation.1 | async-start | bytes 1966080 | tf_op jit(solution)/shard_map/all_gather | solution.py:34
  8.3 191.4 %all-gather.6.cloned.1.call-start = ((), (), s32[]{:S(2)}) async-start(), calls=%async_computation.2 | async-start | bytes 7864320 | tf_op jit(solution)/shard_map/all_gather | solution.py:9
  44.0 110.4 %all-to-all-start = ((bf16[32,1,64,2,256]{4,3,2,1,0:T(2,128)(2,1)}), bf16[32,1,64,2,256]{4,3,2,1,0:T(2,128)(2,1)S(1)}, u32[]{:S(2)}, u32[]{:S(2)}) async-start(bf16[32,1,64,2,256]{4,3,2,1,0:T(2,128)(2,1)} %param.3), calls=%async_computation | async-start | bytes 4194304 | tf_op jit(solution)/shard_map/all_to_all | solution.py:56
  207.3 1.2 copy-start
  355.2 1.9 copy-start.1
Sparse Core Ops, SparseCore 0:
  9.2 33.5 all-gather.3
  44.3 155.3 all-gather.5
